TPU v7x, 32 devices: a whole 2x2x4 slice. The times are simulated.
32 devices in a mesh: dp: 16 (over z, y, x), tensor: 2 (over core).
Axes of the slice: x: 2, y: 2, z: 4, core: 2. Of those that a mesh axis runs over, the one named last changes fastest.
Arguments:
- tokens: bfloat16 [16384, 768], P('dp'), may hold values from -6 to 6
- cotangent: bfloat16 [16384, 768], P('dp'), may hold values from -6 to 6
- lengths: int32 [32], P('dp'), may hold values from 113 to 512, as said below
- proj_weight: float32 [2, 768, 3, 768], P(None, 'dp', None, 'tensor'), may hold values from -0.21875 to 0.21875
- out_weight: float32 [2, 768, 768], P(None, 'dp', 'tensor'), may hold values from -0.875 to 0.875
- up_weight: float32 [2, 768, 3072], P(None, 'dp', 'tensor'), may hold values from -0.21875 to 0.21875
- down_weight: float32 [2, 768, 3072], P(None, 'dp', 'tensor'), may hold values from -0.109375 to 0.109375
- small_params: float32 [2, 8448], replicated, may hold values from -0.8 to 1.4
- proj_first: float32 [2, 768, 3, 768], P(None, 'dp', None, 'tensor'), may hold values from -0.00018310547 to 0.00018310547
- proj_second: float32 [2, 768, 3, 768], P(None, 'dp', None, 'tensor'), may hold values from 3.527916e-11 to 3.52791626e-09
- out_first: float32 [2, 768, 768], P(None, 'dp', 'tensor'), may hold values from -0.00018310547 to 0.00018310547
- out_second: float32 [2, 768, 768], P(None, 'dp', 'tensor'), may hold values from 7.0558325e-12 to 7.0558325e-10
- up_first: float32 [2, 768, 3072], P(None, 'dp', 'tensor'), may hold values from -0.00018310547 to 0.00018310547
- up_second: float32 [2, 768, 3072], P(None, 'dp', 'tensor'), may hold values from 3.527916e-11 to 3.52791626e-09
- down_first: float32 [2, 768, 3072], P(None, 'dp', 'tensor'), may hold values from -0.00018310547 to 0.00018310547
- down_second: float32 [2, 768, 3072], P(None, 'dp', 'tensor'), may hold values from 3.527916e-11 to 3.52791626e-09
- small_first: float32 [2, 8448], replicated, may hold values from -0.00018310547 to 0.00018310547
- small_second: float32 [2, 8448], replicated, may hold values from 3.527916e-11 to 5.644666e-10
Outputs:
- activations: float32 [16384, 768], P('dp')
- input_grad: float32 [16384, 768], P('dp')
- grad_norm: float32 [], replicated
- proj_first_new: float32 [2, 768, 3, 768], P(None, 'dp', None, 'tensor')
- proj_second_new: float32 [2, 768, 3, 768], P(None, 'dp', None, 'tensor')
- proj_weight_new: float32 [2, 768, 3, 768], P(None, 'dp', None, 'tensor')
- out_first_new: float32 [2, 768, 768], P(None, 'dp', 'tensor')
- out_second_new: float32 [2, 768, 768], P(None, 'dp', 'tensor')
- out_weight_new: float32 [2, 768, 768], P(None, 'dp', 'tensor')
- up_first_new: float32 [2, 768, 3072], P(None, 'dp', 'tensor')
- up_second_new: float32 [2, 768, 3072], P(None, 'dp', 'tensor')
- up_weight_new: float32 [2, 768, 3072], P(None, 'dp', 'tensor')
- down_first_new: float32 [2, 768, 3072], P(None, 'dp', 'tensor')
- down_second_new: float32 [2, 768, 3072], P(None, 'dp', 'tensor')
- down_weight_new: float32 [2, 768, 3072], P(None, 'dp', 'tensor')
- small_first_new: float32 [2, 8448], replicated
- small_second_new: float32 [2, 8448], replicated
- small_params_new: float32 [2, 8448], replicated
Inputs may be any that keep to these rules, and one draw needn't show every extreme that they name: `lengths`: each length is 512, 256 or 128, reduced by less than max(1, 16); the first sequence has length 512.
All inputs are finite; a program needn't handle non-finite values.
Results may differ from a plain program's by a relative error of at most 0.03.
The roundings to bfloat16 on the way count: a program that leaves them out, or rounds other values in their place, can miss the bound.
Values may be sent and summed in bfloat16 or wider, within the bound.
No kernel may reach another device: no remote copies, remote signals or barrier semaphores. Data moves between devices by JAX's collectives and lax.ppermute only.
A program may use at most 192 MiB of HBM per device.

v0:
```python
from functools import partial
import math
import jax
import jax.numpy as jnp
from jax import lax
from jax.sharding import PartitionSpec as P

D = 768
HEADS = 12
FF = 3072
beta_one = 0.9
beta_two = 0.999
adam_eps = 1e-06
decay_rate = 0.01
matrix_rate = 1.0
vector_rate = 0.3
clip_norm = 1.0
step_count = 10.0
norm_eps = 1e-06
masked_score = -1e30


def layer_norm(values, norm_gain, norm_shift):
    average = jnp.mean(values, axis=-1, keepdims=True)
    centered = values - average
    variance = jnp.mean(centered * centered, axis=-1, keepdims=True)
    return centered * lax.rsqrt(variance + norm_eps) * norm_gain + norm_shift


def split_vector(packed):
    bounds = [0, D, 2 * D, 2 * D + FF, 3 * D + FF, 4 * D + FF, 5 * D + FF, 6 * D + FF, 7 * D + FF]
    return [packed[bounds[place] : bounds[place + 1]] for place in range(8)]


def head_scores(query, keys, score_scale):
    return jnp.einsum("qhe,khe->hqk", query, keys, preferred_element_type=jnp.float32) * score_scale


def total_scores(pairs, score_scale):
    score_total = head_scores(pairs[0], pairs[1], score_scale)
    for place in range(2, len(pairs), 2):
        score_total = score_total + head_scores(pairs[place], pairs[place + 1], score_scale)
    return score_total


def attend_forward(block_item, score_scale):
    key_valid, value_rows = (block_item[0], block_item[1])
    score_total = total_scores(block_item[2:], score_scale)
    masked = jnp.where(key_valid[None, None, :], score_total, masked_score)
    row_max = jnp.max(masked, axis=-1, keepdims=True)
    exp_terms = jnp.exp(masked - row_max)
    row_sum = jnp.sum(exp_terms, axis=-1, keepdims=True)
    soft_low = (exp_terms / row_sum).astype(jnp.bfloat16)
    context = jnp.einsum("hqk,khe->qhe", soft_low, value_rows, preferred_element_type=jnp.float32)
    return (context.astype(jnp.bfloat16), (row_max + jnp.log(row_sum))[..., 0])


def attend_backward(block_item, score_scale, with_later, keep_total):
    key_valid, value_rows, log_norm, context_grad = (
        block_item[0],
        block_item[1],
        block_item[2],
        block_item[3],
    )
    rest = block_item[4:]
    if with_later:
        later = rest[0]
        pairs = rest[1:]
    else:
        pairs = rest
    score_total = total_scores(pairs, score_scale)
    soft = jnp.where(key_valid[None, None, :], jnp.exp(score_total - log_norm[..., None]), 0.0)
    soft_grad = jnp.einsum(
        "qhe,khe->hqk", context_grad, value_rows, preferred_element_type=jnp.float32
    )
    total_grad = soft * (soft_grad - jnp.sum(soft * soft_grad, axis=-1, keepdims=True))
    if with_later:
        total_grad = total_grad + later
    total_low = total_grad.astype(jnp.bfloat16)
    query_grad = (
        jnp.einsum("hqk,khe->qhe", total_low, pairs[1], preferred_element_type=jnp.float32)
        * score_scale
    )
    key_grad = (
        jnp.einsum("hqk,qhe->khe", total_low, pairs[0], preferred_element_type=jnp.float32)
        * score_scale
    )
    value_grad = jnp.einsum(
        "hqk,qhe->khe", soft.astype(jnp.bfloat16), context_grad, preferred_element_type=jnp.float32
    )
    results = (query_grad, key_grad, value_grad)
    if keep_total:
        results = results + (total_grad,)
    return results


def adam_parts(gradient, first, second, factor):
    clipped = gradient * factor
    first_new = beta_one * first + (1.0 - beta_one) * clipped
    second_new = beta_two * second + (1.0 - beta_two) * clipped * clipped
    first_hat = first_new / (1.0 - beta_one**step_count)
    second_hat = second_new / (1.0 - beta_two**step_count)
    return (first_new, second_new, first_hat / (jnp.sqrt(second_hat) + adam_eps))


def local(
    tokens,
    cotangent,
    lengths,
    proj_weight,
    out_weight,
    up_weight,
    down_weight,
    small_params,
    proj_first,
    proj_second,
    out_first,
    out_second,
    up_first,
    up_second,
    down_first,
    down_second,
    small_first,
    small_second,
):
    layers = proj_weight.shape[0]
    seq_count = lengths.shape[0]
    seq_len = tokens.shape[0] // seq_count
    local_width = proj_weight.shape[3]
    head_dim = D // HEADS
    local_heads = local_width // head_dim
    hidden_local = up_weight.shape[2]
    score_scale = 1.0 / math.sqrt(head_dim)
    share_scale = 1.0 / lax.axis_size("tensor")
    tensor_rank = lax.axis_index("tensor")
    proj_full, out_full, up_full, down_full = (
        lax.all_gather(proj_weight.astype(jnp.bfloat16), "dp", axis=1, tiled=True),
        lax.all_gather(out_weight.astype(jnp.bfloat16), "dp", axis=1, tiled=True),
        lax.all_gather(up_weight.astype(jnp.bfloat16), "dp", axis=1, tiled=True),
        lax.all_gather(down_weight.astype(jnp.bfloat16), "dp", axis=1, tiled=True),
    )
    positions = jnp.arange(seq_len)
    key_valid = positions[None, :] < lengths[:, None]
    row_valid = key_valid.reshape(-1, 1)

    def own_part(vector, width):
        return lax.dynamic_slice_in_dim(vector, tensor_rank * width, width)

    def place_part(local_values, full_width):
        return lax.dynamic_update_slice_in_dim(
            jnp.zeros((full_width,), jnp.float32),
            local_values,
            tensor_rank * local_values.shape[0],
            0,
        )

    def heads_view(rows):
        return rows.reshape(seq_count, seq_len, local_heads, head_dim)

    hidden = tokens.astype(jnp.float32)
    saved = []
    for layer_at in range(layers):
        bias_v, bias_o, bias_up, bias_down, gain_one, shift_one, gain_two, shift_two = split_vector(
            small_params[layer_at]
        )
        input_low = hidden.astype(jnp.bfloat16)
        projected = jnp.einsum(
            "td,dcf->tcf", input_low, proj_full[layer_at], preferred_element_type=jnp.float32
        )
        query_low = projected[:, 0].astype(jnp.bfloat16)
        key_low = projected[:, 1].astype(jnp.bfloat16)
        value_low = (projected[:, 2] + own_part(bias_v, local_width)).astype(jnp.bfloat16)
        pairs = [heads_view(query_low), heads_view(key_low)]
        for earlier in reversed(saved):
            pairs += [heads_view(earlier["query"]), heads_view(earlier["keys"])]
        context_low, log_norm = lax.map(
            partial(attend_forward, score_scale=score_scale),
            (key_valid, heads_view(value_low)) + tuple(pairs),
        )
        context_low = context_low.reshape(-1, local_width)
        attended = lax.psum(
            jnp.einsum(
                "tf,df->td", context_low, out_full[layer_at], preferred_element_type=jnp.float32
            ).astype(jnp.bfloat16),
            "tensor",
        ).astype(jnp.float32)
        first_in = hidden + attended + bias_o
        first_out = layer_norm(first_in, gain_one, shift_one)
        first_low = first_out.astype(jnp.bfloat16)
        before_act = jnp.einsum(
            "td,df->tf", first_low, up_full[layer_at], preferred_element_type=jnp.float32
        ) + own_part(bias_up, hidden_local)
        act_low = jax.nn.gelu(before_act, approximate=False).astype(jnp.bfloat16)
        returned = lax.psum(
            jnp.einsum(
                "tf,df->td", act_low, down_full[layer_at], preferred_element_type=jnp.float32
            ).astype(jnp.bfloat16),
            "tensor",
        ).astype(jnp.float32)
        second_in = first_out + returned + bias_down
        saved.append(
            {
                "layer_input": input_low,
                "query": query_low,
                "keys": key_low,
                "value_rows": value_low,
                "log_norm": log_norm,
                "context": context_low,
                "first_in": first_in,
                "first_low": first_low,
                "before_act": before_act,
                "act_low": act_low,
                "second_in": second_in,
            }
        )
        hidden = layer_norm(second_in, gain_two, shift_two)
    grad_rows = jnp.where(row_valid, cotangent.astype(jnp.float32), 0.0)
    proj_grads = [None] * layers
    out_grads = [None] * layers
    up_grads = [None] * layers
    down_grads = [None] * layers
    small_grads = [None] * layers
    later_total = None
    for layer_at in reversed(range(layers)):
        kept = saved[layer_at]
        bias_v, bias_o, bias_up, bias_down, gain_one, shift_one, gain_two, shift_two = split_vector(
            small_params[layer_at]
        )
        second_in_grad, gain_two_grad, shift_two_grad = jax.vjp(
            layer_norm, kept["second_in"], gain_two, shift_two
        )[1](grad_rows)
        down_in_low = second_in_grad.astype(jnp.bfloat16)
        down_grads[layer_at] = jnp.einsum(
            "td,tf->df", down_in_low, kept["act_low"], preferred_element_type=jnp.float32
        )
        act_grad = jnp.einsum(
            "td,df->tf", down_in_low, down_full[layer_at], preferred_element_type=jnp.float32
        )
        before_grad = jax.vjp(partial(jax.nn.gelu, approximate=False), kept["before_act"])[1](
            act_grad
        )[0]
        before_low = before_grad.astype(jnp.bfloat16)
        up_grads[layer_at] = jnp.einsum(
            "td,tf->df", kept["first_low"], before_low, preferred_element_type=jnp.float32
        )
        first_back = lax.psum(
            jnp.einsum(
                "tf,df->td", before_low, up_full[layer_at], preferred_element_type=jnp.float32
            ).astype(jnp.bfloat16),
            "tensor",
        ).astype(jnp.float32)
        first_out_grad = second_in_grad + first_back
        first_in_grad, gain_one_grad, shift_one_grad = jax.vjp(
            layer_norm, kept["first_in"], gain_one, shift_one
        )[1](first_out_grad)
        out_in_low = first_in_grad.astype(jnp.bfloat16)
        out_grads[layer_at] = jnp.einsum(
            "td,tf->df", out_in_low, kept["context"], preferred_element_type=jnp.float32
        )
        context_grad = jnp.einsum(
            "td,df->tf", out_in_low, out_full[layer_at], preferred_element_type=jnp.float32
        ).astype(jnp.bfloat16)
        pairs = [heads_view(kept["query"]), heads_view(kept["keys"])]
        for earlier in reversed(saved[:layer_at]):
            pairs += [heads_view(earlier["query"]), heads_view(earlier["keys"])]
        items = (
            key_valid,
            heads_view(kept["value_rows"]),
            kept["log_norm"],
            heads_view(context_grad),
        )
        with_later = later_total is not None
        if with_later:
            items = items + (later_total,)
        items = items + tuple(pairs)
        results = lax.map(
            partial(
                attend_backward,
                score_scale=score_scale,
                with_later=with_later,
                keep_total=layer_at > 0,
            ),
            items,
        )
        later_total = results[3] if layer_at > 0 else None
        query_grad = results[0].reshape(-1, local_width)
        key_grad = results[1].reshape(-1, local_width)
        value_grad = results[2].reshape(-1, local_width)
        proj_grad_low = jnp.stack([query_grad, key_grad, value_grad], axis=1).astype(jnp.bfloat16)
        proj_grads[layer_at] = jnp.einsum(
            "td,tcf->dcf", kept["layer_input"], proj_grad_low, preferred_element_type=jnp.float32
        )
        input_back = lax.psum(
            jnp.einsum(
                "tcf,dcf->td",
                proj_grad_low,
                proj_full[layer_at],
                preferred_element_type=jnp.float32,
            ).astype(jnp.bfloat16),
            "tensor",
        ).astype(jnp.float32)
        grad_rows = first_in_grad + input_back
        small_grads[layer_at] = jnp.concatenate(
            [
                place_part(jnp.sum(value_grad, axis=0), D),
                share_scale * jnp.sum(first_in_grad, axis=0),
                place_part(jnp.sum(before_grad, axis=0), FF),
                share_scale * jnp.sum(second_in_grad, axis=0),
                share_scale * gain_one_grad,
                share_scale * shift_one_grad,
                share_scale * gain_two_grad,
                share_scale * shift_two_grad,
            ]
        )
    big_totals = (
        jnp.stack(proj_grads),
        jnp.stack(out_grads),
        jnp.stack(up_grads),
        jnp.stack(down_grads),
    )
    small_partial = jnp.stack(small_grads)
    row_count = proj_weight.shape[1]
    summed = lax.psum((big_totals[0], big_totals[1], big_totals[2], big_totals[3]), "dp")
    row_start = lax.axis_index("dp") * row_count
    shares = tuple(
        (lax.dynamic_slice_in_dim(summed_part, row_start, row_count, 1) for summed_part in summed)
    )
    masters = (proj_weight, out_weight, up_weight, down_weight)
    firsts = (proj_first, out_first, up_first, down_first)
    seconds = (proj_second, out_second, up_second, down_second)
    square_part = jnp.sum(shares[0] * shares[0])
    for kind_at in range(1, 4):
        square_part = square_part + jnp.sum(shares[kind_at] * shares[kind_at])
    weight_square = jnp.stack(
        [jnp.sum(master * master, axis=tuple(range(1, master.ndim))) for master in masters]
    )
    square_big, weight_square, small_grad = lax.psum(
        (square_part, weight_square, small_partial), ("dp", "tensor")
    )
    grad_norm = jnp.sqrt(square_big + jnp.sum(small_grad * small_grad))
    factor = clip_norm / jnp.maximum(grad_norm, clip_norm)
    moments = []
    updates = []
    for kind_at in range(4):
        first_new, second_new, direction = adam_parts(
            shares[kind_at], firsts[kind_at], seconds[kind_at], factor
        )
        moments.append((first_new, second_new))
        updates.append(direction + decay_rate * masters[kind_at])
    update_square = jnp.stack(
        [jnp.sum(update * update, axis=tuple(range(1, update.ndim))) for update in updates]
    )
    update_square = lax.psum(update_square, ("dp", "tensor"))
    ratio = jnp.sqrt(weight_square) / jnp.sqrt(update_square)
    outputs = [hidden, grad_rows, grad_norm]
    for kind_at in range(4):
        master = masters[kind_at]
        scaled = ratio[kind_at].reshape((-1,) + (1,) * (master.ndim - 1))
        outputs += [
            moments[kind_at][0],
            moments[kind_at][1],
            master - matrix_rate * scaled * updates[kind_at],
        ]
    small_first_new, small_second_new, small_direction = adam_parts(
        small_grad, small_first, small_second, factor
    )
    outputs += [small_first_new, small_second_new, small_params - vector_rate * small_direction]
    return tuple(outputs)


def solution(mesh):
    placed = (
        P("dp", None),
        P("dp", None),
        P("dp"),
        P(None, "dp", None, "tensor"),
        P(None, "dp", "tensor"),
        P(None, "dp", "tensor"),
        P(None, "dp", "tensor"),
        P(),
        P(None, "dp", None, "tensor"),
        P(None, "dp", None, "tensor"),
        P(None, "dp", "tensor"),
        P(None, "dp", "tensor"),
        P(None, "dp", "tensor"),
        P(None, "dp", "tensor"),
        P(None, "dp", "tensor"),
        P(None, "dp", "tensor"),
        P(),
        P(),
    )
    return jax.shard_map(
        local,
        mesh=mesh,
        in_specs=placed,
        out_specs=(
            P("dp", None),
            P("dp", None),
            P(),
            P(None, "dp", None, "tensor"),
            P(None, "dp", None, "tensor"),
            P(None, "dp", None, "tensor"),
            P(None, "dp", "tensor"),
            P(None, "dp", "tensor"),
            P(None, "dp", "tensor"),
            P(None, "dp", "tensor"),
            P(None, "dp", "tensor"),
            P(None, "dp", "tensor"),
            P(None, "dp", "tensor"),
            P(None, "dp", "tensor"),
            P(None, "dp", "tensor"),
            P(),
            P(),
            P(),
        ),
        check_vma=False,
    )
```

profile of v0, /device:TPU:0, one launch (start us, length us, event | category | flops | bytes accessed | tf_op | source)
XLA Modules:
  0.0 1741.2 jit_solution(10675762374318251473)
XLA Ops:
  13.1 72.2 %all-gather.5.cloned.1.call-done = bf16[2,768,3,384]{3,1,2,0:T(8,128)(2,1)} async-done(((bf16[2,48,3,384]{3,1,2,0:T(8,128)(2,1)}), bf16[2,768,3,384]{3,1,2,0:T(8,128)(2,1)}) %all-gather.5.cloned.1.call-update) | async-done | bytes 3538960 | tf_op jit(solution)/shard_map/all_gather | solution.py:137
  85.3 5.6 fusion.209
  103.5 11.4 while.54
  116.8 26.5 %all-gather.7.cloned.1.call-done = bf16[2,768,384]{2,1,0:T(8,128)(2,1)} async-done(((bf16[2,48,384]{2,1,0:T(8,128)(2,1)}), bf16[2,768,384]{2,1,0:T(8,128)(2,1)}) %all-gather.7.cloned.1.call-update) | async-done | bytes 1179664 | tf_op jit(solution)/shard_map/all_gather | solution.py:138
  150.6 15.8 all-reduce.13.cloned.1.call-done
  169.4 82.1 %all-gather.9.cloned.1.call-done = bf16[2,768,1536]{2,1,0:T(8,128)(2,1)} async-done(((bf16[2,48,1536]{2,1,0:T(8,128)(2,1)}), bf16[2,768,1536]{2,1,0:T(8,128)(2,1)}) %all-gather.9.cloned.1.call-update) | async-done | bytes 4718608 | tf_op jit(solution)/shard_map/all_gather | solution.py:139
  251.5 20.8 %multiply_convert_fusion.1 = (bf16[1024,1536]{1,0:T(8,128)(2,1)}, f32[1024,1536]{1,0:T(8,128)}, f32[1024,1536]{1,0:T(8,128)}) fusion(f32[1536]{0:T(1024)S(1)} %dynamic-slice_reduce_fusion.5, bf16[2,768,1536]{2,1,0:T(8,128)(2,1)} %all-gather.9.cloned.1.call-done, f32[768]{0:T(1024)S(1)} %get-tuple-element.431, f32[768]{0:T(1024)S(1)} %get-tuple-element.432, ...), kind=kOutput, calls=%fused_computation.155 | convolution fusion | flops 2526806016 | bytes 21257216 | tf_op jit(solution)/shard_map/td,df->tf/dot_general | solution.py:190
  272.3 61.6 %all-gather.11.cloned.1.call-done = bf16[2,768,1536]{2,1,0:T(8,128)(2,1)} async-done(((bf16[2,48,1536]{2,1,0:T(8,128)(2,1)}), bf16[2,768,1536]{2,1,0:T(8,128)(2,1)}) %all-gather.11.cloned.1.call-update) | async-done | bytes 4718608 | tf_op jit(solution)/shard_map/all_gather | solution.py:140
  333.9 6.4 fusion.151
  340.5 19.1 %all-reduce.15.cloned.1.call-done = bf16[1024,768]{1,0:T(8,128)(2,1)} async-done(((bf16[1024,768]{1,0:T(8,128)(2,1)}), bf16[1024,768]{1,0:T(8,128)(2,1)}) %all-reduce.15.cloned.1.call-update) | async-done | bytes 1572880 | tf_op jit(solution)/shard_map/psum | solution.py:194
  363.7 3.8 fusion.210
  380.8 14.3 while.55
  400.4 21.7 %all-reduce.17.cloned.1.call-done = bf16[1024,768]{1,0:T(8,128)(2,1)} async-done(((bf16[1024,768]{1,0:T(8,128)(2,1)}), bf16[1024,768]{1,0:T(8,128)(2,1)}) %all-reduce.17.cloned.1.call-update) | async-done | bytes 1572880 | tf_op jit(solution)/shard_map/psum | solution.py:181
  426.5 18.6 %multiply_convert_fusion = (bf16[1024,1536]{1,0:T(8,128)(2,1)S(1)}, f32[1024,1536]{1,0:T(8,128)}, f32[1024,1536]{1,0:T(8,128)}) fusion(f32[1536]{0:T(1024)S(1)} %dynamic-slice_reduce_fusion.4, bf16[2,768,1536]{2,1,0:T(8,128)(2,1)S(1)} %bitcast.417, f32[1024,768]{1,0:T(8,128)S(1)} %get-tuple-element.545, f32[768]{0:T(1024)S(1)} %copy-done.104, ...), kind=kOutput, calls=%fused_computation.142 | convolution fusion | flops 2523660288 | bytes 21258240 | tf_op jit(solution)/shard_map/td,df->tf/dot_general | solution.py:190
  446.8 5.4 fusion.149
  452.2 21.7 %all-reduce.19.cloned.1.call-done = bf16[1024,768]{1,0:T(8,128)(2,1)} async-done(((bf16[1024,768]{1,0:T(8,128)(2,1)}), bf16[1024,768]{1,0:T(8,128)(2,1)}) %all-reduce.19.cloned.1.call-update) | async-done | bytes 1572880 | tf_op jit(solution)/shard_map/psum | solution.py:194
  484.4 9.5 fusion.211
  495.6 3.7 fusion.150
  503.6 8.0 convolution_bitcast_fusion.2
  511.6 9.5 all-reduce.21.cloned.1.call-done
  521.1 4.9 multiply_reduce_fusion.3
  541.2 36.4 %while.56 = (s32[]{:T(128)}, bf16[2,512,6,64]{1,3,2,0:T(8,128)(2,1)}, bf16[2,512,6,64]{1,3,2,0:T(8,128)(2,1)}, f32[2,512,6,64]{1,3,2,0:T(8,128)}, f32[2,6,512,51...) while((s32[]{:T(128)}, ...), condition=%wide.region_27.28_spmd, body=%wide.region_25.27_spmd.sunk | while | flops 1227224064 | bytes 94064864 | solution.py:276
  548.1 4.2 bitcast_dynamic-update-slice_fusion.8
  566.1 4.3 bitcast_dynamic-update-slice_fusion.8
  592.2 5.6 bitcast_convert_fusion.1
  598.0 7.9 convolution_bitcast_fusion
  608.8 4.3 convolution_bitcast_fusion.4
  613.1 6.5 all-reduce.23.cloned.1.call-done
  619.7 5.1 multiply_reduce_fusion.4
  627.1 9.6 fusion.212
  638.3 3.7 fusion.152
  642.1 5.6 convolution_bitcast_fusion.1
  647.8 7.4 pad_maximum_fusion.1
  655.3 4.9 convolution_bitcast_fusion.3
  663.8 4.8 multiply_reduce_fusion.5
  676.7 54.2 %while.57 = (s32[]{:T(128)}, bf16[2,512,6,64]{1,3,2,0:T(8,128)(2,1)}, bf16[2,512,6,64]{1,3,2,0:T(8,128)(2,1)}, f32[2,512,6,64]{1,3,2,0:T(8,128)}, bf16[2,512,6,6...) while((s32[]{:T(128)}, ...), condition=%wide.region_36.37_spmd, body=%wide.region_34.36_spmd.sunk | while | flops 1222512128 | bytes 87736576 | solution.py:276
  676.7 5.2 exponential_select_fusion.3
  681.9 7.6 fusion.310
  689.5 7.8 fusion.311
  703.8 5.2 exponential_select_fusion.3
  709.0 7.6 fusion.310
  716.6 7.8 fusion.311
  739.8 5.2 bitcast_convert_fusion
  745.3 8.5 pad_maximum_fusion
  772.1 736.8 %all-reduce.31.cloned.1.call-done = (f32[2,768,3,384]{3,1,2,0:T(8,128)}, f32[2,768,384]{2,1,0:T(8,128)}, f32[2,768,1536]{2,1,0:T(8,128)}, f32[2,768,1536]{2,1,0:T(8,128)}) async-done(((f32[2,768,3,384]{3,1,2,0:T(8,128)}, f32[2,768,384]{2,1,0:T(8,128)}, f32[2,768,1536]{2,1,0:T(8,128)}, f32[2,768,1536]{2,1,0:T(8,128)}), (f32[2,768,3,384]{3,1,2,0:T(8,128)}, f32[2,768,384]{2,1,0:T(8,128)}, ...) | async-done | bytes 28311568 | tf_op jit(solution)/shard_map/psum | solution.py:323
  1518.5 114.0 %all-reduce.29.cloned.1.call-done = f32[2,8448]{1,0:T(2,128)} async-done(((f32[2,8448]{1,0:T(2,128)}), f32[2,8448]{1,0:T(2,128)}) %all-reduce.29.cloned.1.call-update) | async-done | bytes 67600 | tf_op jit(solution)/shard_map/psum | solution.py:337
  1634.1 42.6 %psum.124 = f32[]{:T(128)} all-reduce(f32[]{:T(128)S(6)} %add.424), channel_id=1, replica_groups=mesh['dp'=16,'tensor'=2] {'dp','tensor'}, use_global_device_ids=true, to_apply=%region_46.47 | all-reduce | flops 1 | bytes 8 | tf_op jit(solution)/shard_map/psum | solution.py:337
  1687.8 39.3 %all-reduce = (f32[4,2]{1,0:T(4,128)S(1)}, f32[4,2]{1,0:T(4,128)S(1)}) all-reduce(f32[4,2]{1,0:T(4,128)S(1)} %pad_maximum_fusion.12, f32[4,2]{1,0:T(4,128)S(1)} %pad_maximum_fusion.11), channel_id=1, replica_groups=mesh['dp'=16,'tensor'=2] {'dp','tensor'}, use_global_device_ids=true, to_apply=%region_74.75 | all-reduce | flops 16 | bytes 128 | tf_op jit(solution)/shard_map/psum | solution.py:353
  (542 shorter events, 240.5 us)
Async XLA Ops:
  7.2 78.1 %all-gather.5.cloned.1.call-start = ((), (), s32[]{:S(2)}) async-start(), calls=%async_computation | async-start | bytes 3760128 | tf_op jit(solution)/shard_map/all_gather | solution.py:137
  9.0 134.3 %all-gather.7.cloned.1.call-start = ((), (), s32[]{:S(2)}) async-start(), calls=%async_computation.1 | async-start | bytes 1253376 | tf_op jit(solution)/shard_map/all_gather | solution.py:138
  10.6 155.7 %all-reduce.13.cloned.1.call-start = ((), (), s32[]{:S(2)}) async-start(), calls=%async_computation.2 | async-start | bytes 3145728 | tf_op jit(solution)/shard_map/psum | solution.py:181
  12.2 347.3 %copy-start.73 = (f32[768]{0:T(1024)}, f32[768]{0:T(1024)S(1)}, u32[]{:S(2)}) copy-start(f32[768]{0:T(1024)S(1)} %get-tuple-element.433) | copy-start | bytes 9220
  12.2 347.3 %copy-start.82 = (f32[768]{0:T(1024)}, f32[768]{0:T(1024)S(1)}, u32[]{:S(2)}) copy-start(f32[768]{0:T(1024)S(1)} %get-tuple-element.432) | copy-start | bytes 9220
  12.2 347.3 %copy-start.100 = (f32[768]{0:T(1024)}, f32[768]{0:T(1024)S(1)}, u32[]{:S(2)}) copy-start(f32[768]{0:T(1024)S(1)} %get-tuple-element.431) | copy-start | bytes 9220
  12.2 409.8 %copy-start.86 = (f32[768]{0:T(1024)}, f32[768]{0:T(1024)S(1)}, u32[]{:S(2)}) copy-start(f32[768]{0:T(1024)S(1)} %get-tuple-element.429) | copy-start | bytes 9220
  12.2 409.8 %copy-start.102 = (f32[768]{0:T(1024)}, f32[768]{0:T(1024)S(1)}, u32[]{:S(2)}) copy-start(f32[768]{0:T(1024)S(1)} %get-tuple-element.428) | copy-start | bytes 9220
  114.9 28.3 %copy-start.20 = (bf16[2,512,6,64]{1,3,2,0:T(8,128)(2,1)}, bf16[2,512,6,64]{1,3,2,0:T(8,128)(2,1)S(1)}, u32[]{:S(2)}) copy-start(bf16[2,512,6,64]{1,3,2,0:T(8,128)(2,1)S(1)} %get-tuple-element.1014) | copy-start | bytes 2359300
  114.9 31.9 %copy-start.69 = (f32[2,6,512]{2,1,0:T(8,128)}, f32[2,6,512]{2,1,0:T(8,128)S(1)}, u32[]{:S(2)}) copy-start(f32[2,6,512]{2,1,0:T(8,128)S(1)} %get-tuple-element.954) | copy-start | bytes 73732
  116.8 32.0 %copy-start.32 = (f32[2,48,1536]{2,1,0:T(8,128)S(1)}, f32[2,48,1536]{2,1,0:T(8,128)}, u32[]{:S(2)}) copy-start(f32[2,48,1536]{2,1,0:T(8,128)} %param.32) | copy-start | bytes 1769476
  143.3 23.1 %copy-start.10 = (bf16[1024,768]{1,0:T(8,128)(2,1)S(1)}, bf16[1024,768]{1,0:T(8,128)(2,1)}, u32[]{:S(2)}) copy-start(bf16[1024,768]{1,0:T(8,128)(2,1)} %param.26) | copy-start | bytes 4718596
  146.9 104.6 %all-gather.9.cloned.1.call-start = ((), (), s32[]{:S(2)}) async-start(), calls=%async_computation.3 | async-start | bytes 5013504 | tf_op jit(solution)/shard_map/all_gather | solution.py:139
  148.8 185.2 %all-gather.11.cloned.1.call-start = ((), (), s32[]{:S(2)}) async-start(), calls=%async_computation.4 | async-start | bytes 5013504 | tf_op jit(solution)/shard_map/all_gather | solution.py:140
  149.6 209.9 %all-reduce.15.cloned.1.call-start = ((), (), s32[]{:S(2)}) async-start(), calls=%async_computation.5 | async-start | bytes 3145728 | tf_op jit(solution)/shard_map/psum | solution.py:194
  150.5 100.9 %copy-start.116 = (f32[1536]{0:T(1024)}, f32[1536]{0:T(1024)S(1)}, u32[]{:S(2)}) copy-start(f32[1536]{0:T(1024)S(1)} %dynamic-slice_reduce_fusion.5) | copy-start | bytes 18436
  168.5 191.1 %copy-start.76 = (f32[1024]{0:T(1024)}, f32[1024]{0:T(1024)S(1)}, u32[]{:S(2)}) copy-start(f32[1024]{0:T(1024)S(1)} %broadcast_multiply_fusion.3) | copy-start | bytes 12292
  169.4 102.9 %copy-start.92 = (f32[1024]{0:T(1024)}, f32[1024]{0:T(1024)S(1)}, u32[]{:S(2)}) copy-start(f32[1024]{0:T(1024)S(1)} %multiply_reduce_fusion.13) | copy-start | bytes 12292
  169.4 190.2 %copy-start.84 = (f32[1024]{0:T(1024)}, f32[1024]{0:T(1024)S(1)}, u32[]{:S(2)}) copy-start(f32[1024]{0:T(1024)S(1)} %fusion.167) | copy-start | bytes 12292
  340.4 81.7 %all-reduce.17.cloned.1.call-start = ((), (), s32[]{:S(2)}) async-start(), calls=%async_computation.6 | async-start | bytes 3145728 | tf_op jit(solution)/shard_map/psum | solution.py:181
  363.2 58.9 %copy-start.78 = (f32[1024]{0:T(1024)}, f32[1024]{0:T(1024)S(1)}, u32[]{:S(2)}) copy-start(f32[1024]{0:T(1024)S(1)} %broadcast_multiply_fusion.2) | copy-start | bytes 12292
  363.7 58.4 %copy-start.89 = (f32[1024]{0:T(1024)}, f32[1024]{0:T(1024)S(1)}, u32[]{:S(2)}) copy-start(f32[1024]{0:T(1024)S(1)} %fusion.168) | copy-start | bytes 12292
  397.1 25.0 %copy-start.106 = (f32[768]{0:T(1024)S(1)}, f32[768]{0:T(1024)}, u32[]{:S(2)}) copy-start(f32[768]{0:T(1024)} %get-tuple-element.427) | copy-start | bytes 9220
  400.3 73.6 %all-reduce.19.cloned.1.call-start = ((), (), s32[]{:S(2)}) async-start(), calls=%async_computation.7 | async-start | bytes 3145728 | tf_op jit(solution)/shard_map/psum | solution.py:194
  425.8 19.4 %copy-start.3 = (f32[1024,768]{1,0:T(8,128)}, f32[1024,768]{1,0:T(8,128)S(1)}, u32[]{:S(2)}) copy-start(f32[1024,768]{1,0:T(8,128)S(1)} %get-tuple-element.545) | copy-start | bytes 9437188
  446.8 27.2 %copy-start.105 = (f32[768]{0:T(1024)S(1)}, f32[768]{0:T(1024)}, u32[]{:S(2)}) copy-start(f32[768]{0:T(1024)} %get-tuple-element.424) | copy-start | bytes 9220
  452.2 68.9 %all-reduce.21.cloned.1.call-start = ((), (), s32[]{:S(2)}) async-start(), calls=%async_computation.8 | async-start | bytes 3145728 | tf_op jit(solution)/shard_map/psum | solution.py:246
  481.4 14.2 slice-start.4
  484.4 11.2 slice-start.5
  499.3 120.3 %all-reduce.23.cloned.1.call-start = ((), (), s32[]{:S(2)}) async-start(), calls=%async_computation.9 | async-start | bytes 3145728 | tf_op jit(solution)/shard_map/psum | solution.py:293
  597.9 65.9 %all-reduce.25.cloned.1.call-start = ((), (), s32[]{:S(2)}) async-start(), calls=%async_computation.10 | async-start | bytes 3145728 | tf_op jit(solution)/shard_map/psum | solution.py:246
  613.1 11.7 copy-start.95
  625.2 13.1 slice-start.6
  627.1 11.3 slice-start.7
  642.1 125.4 %all-reduce.27.cloned.1.call-start = ((), (), s32[]{:S(2)}) async-start(), calls=%async_computation.11 | async-start | bytes 3145728 | tf_op jit(solution)/shard_map/psum | solution.py:293
  681.9 19.8 %slice-start = ((s8[6291456]{0:T(1024)(128)(4,1)}), s8[2097152]{0:T(1024)(128)(4,1)S(1)}, s32[]{:S(2)}) async-start(s8[6291456]{0:T(1024)(128)(4,1)} %bitcast.400), calls=%async_computation.14 | async-start | bytes 4194304 | tf_op jit(solution)/shard_map/while
  689.5 12.2 slice-start.1
  709.0 19.8 %slice-start = ((s8[6291456]{0:T(1024)(128)(4,1)}), s8[2097152]{0:T(1024)(128)(4,1)S(1)}, s32[]{:S(2)}) async-start(s8[6291456]{0:T(1024)(128)(4,1)} %bitcast.400), calls=%async_computation.14 | async-start | bytes 4194304 | tf_op jit(solution)/shard_map/while
  716.6 12.2 slice-start.1
  745.0 763.9 %all-reduce.31.cloned.1.call-start = ((), (), s32[]{:S(2)}) async-start(), calls=%async_computation.13 | async-start | bytes 56623104 | tf_op jit(solution)/shard_map/psum | solution.py:323
  763.9 868.6 %all-reduce.29.cloned.1.call-start = ((), (), s32[]{:S(2)}) async-start(), calls=%async_computation.12 | async-start | bytes 135168 | tf_op jit(solution)/shard_map/psum | solution.py:337
  767.5 910.6 %copy-start.47 = (f32[2,48,384]{2,1,0:T(8,128)S(1)}, f32[2,48,384]{2,1,0:T(8,128)}, u32[]{:S(2)}) copy-start(f32[2,48,384]{2,1,0:T(8,128)} %param.30) | copy-start | bytes 442372
  771.2 908.8 %copy-start.34 = (f32[2,48,1536]{2,1,0:T(8,128)S(1)}, f32[2,48,1536]{2,1,0:T(8,128)}, u32[]{:S(2)}) copy-start(f32[2,48,1536]{2,1,0:T(8,128)} %param.31) | copy-start | bytes 1769476
  771.2 908.8 %copy-start.66 = (f32[2,48,1536]{2,1,0:T(8,128)S(1)}, f32[2,48,1536]{2,1,0:T(8,128)}, u32[]{:S(2)}) copy-start(f32[2,48,1536]{2,1,0:T(8,128)} %param.38) | copy-start | bytes 1769476
  1508.9 173.1 %copy-start.33 = (f32[2,48,1536]{2,1,0:T(8,128)S(1)}, f32[2,48,1536]{2,1,0:T(8,128)}, u32[]{:S(2)}) copy-start(f32[2,48,1536]{2,1,0:T(8,128)} %param.32) | copy-start | bytes 1769476
  1682.0 47.4 %copy-start.42 = (f32[2,48,1536]{2,1,0:T(8,128)}, f32[2,48,1536]{2,1,0:T(8,128)S(1)}, u32[]{:S(2)}) copy-start(f32[2,48,1536]{2,1,0:T(8,128)S(1)} %get-tuple-element.528) | copy-start | bytes 1769476
  1682.0 47.4 %copy-start.43 = (f32[2,48,1536]{2,1,0:T(8,128)}, f32[2,48,1536]{2,1,0:T(8,128)S(1)}, u32[]{:S(2)}) copy-start(f32[2,48,1536]{2,1,0:T(8,128)S(1)} %get-tuple-element.529) | copy-start | bytes 1769476
  1685.2 45.4 %copy-start.44 = (f32[2,48,1536]{2,1,0:T(8,128)}, f32[2,48,1536]{2,1,0:T(8,128)S(1)}, u32[]{:S(2)}) copy-start(f32[2,48,1536]{2,1,0:T(8,128)S(1)} %get-tuple-element.530) | copy-start | bytes 1769476
  (111 other events, 434.2 us)
Sparse Core Ops, SparseCore 0:
  11.3 73.9 all-gather.4
  88.5 54.6 all-gather.6
  147.0 19.2 all-reduce.12
  169.8 81.6 all-gather.8
  255.0 78.9 all-gather.10
  340.5 19.0 all-reduce.14
  400.5 21.5 all-reduce.16
  452.3 21.5 all-reduce.18
  499.5 21.5 all-reduce.20
  598.0 21.5 all-reduce.22
  642.2 21.5 all-reduce.24
  745.1 21.5 all-reduce.26
  773.2 735.7 all-reduce.30
  1515.9 116.6 all-reduce.28
where the time goes:
time: 1750 us; the launch traced here: 1740 us
  waiting for transfers between devices  1190 us (68%)
  matrix products  238 us (14%)
  other arithmetic  120 us (7%)
  local copies, waits for them, and re-layouts  86.9 us (5%)
  blocking collectives  81.9 us (5%)
  between operations  20.9 us (1%)
    psum x1, waiting for transfers between devices, local(): lax.psum((big_totals[0], big_totals[1], big_totals[2], big_totals[3]), 'dp')  737 us
    psum x1, waiting for transfers between devices, local(): lax.psum((square_part, weight_square, small_partial), ('dp', 'tensor'))  114 us
    all_gather x1, waiting for transfers between devices, local(): lax.all_gather(up_weight.astype(jnp.bfloat16), 'dp', axis=1, tiled=True)  82.1 us
    all_gather x1, waiting for transfers between devices, local(): lax.all_gather(proj_weight.astype(jnp.bfloat16), 'dp', axis=1, tiled=True)  72.2 us
    all_gather x1, waiting for transfers between devices, local(): lax.all_gather(down_weight.astype(jnp.bfloat16), 'dp', axis=1, tiled=True)  61.6 us
    psum x1, blocking collectives, local(): lax.psum((square_part, weight_square, small_partial), ('dp', 'tensor'))  42.6 us
    psum x2, waiting for transfers between devices, local(): lax.psum(jnp.einsum('tf,df->td', act_low, down_full[layer_at], preferred_...  40.7 us
    dot_general x2, matrix products, local(): jnp.einsum('td,df->tf', first_low, up_full[layer_at], preferred_element_t...  39.4 us
  transfers between devices with their start and end apart: 14, of which 13 were waited for; matrix products, arithmetic and copies ran while one was open for 8% of the time, Pallas kernels for 0%

commit v1 on v0

--- a/solution.py
+++ b/solution.py
@@ -18,6 +18,28 @@
 step_count = 10.0
 norm_eps = 1e-06
 masked_score = -1e30
+
+
+def in_order(blocks, dim):
+    blocks = jnp.moveaxis(blocks, 0, dim)
+    shape = blocks.shape
+    return blocks.reshape(*shape[:dim], shape[dim] * shape[dim + 1], *shape[dim + 2 :])
+
+
+def ring_gather(x, axis, dim):
+    devices = lax.axis_size(axis)
+    pairs = [(i, (i + 1) % devices) for i in range(devices)]
+    back = [(b, a) for a, b in pairs]
+    lower, upper = ([], [])
+    for step in range(devices - 1):
+        if step % 2 == 0:
+            lower.append(lax.ppermute(lower[-1] if lower else x, axis, pairs))
+        else:
+            upper.append(lax.ppermute(upper[-1] if upper else x, axis, back))
+    blocks = jnp.stack([*lower[::-1], x, *upper])
+    shift = lax.axis_index(axis) - len(lower)
+    blocks = blocks[(jnp.arange(devices) - shift) % devices]
+    return in_order(blocks, dim)
 
 
 def layer_norm(values, norm_gain, norm_shift):
@@ -134,7 +156,7 @@
     share_scale = 1.0 / lax.axis_size("tensor")
     tensor_rank = lax.axis_index("tensor")
     proj_full, out_full, up_full, down_full = (
-        lax.all_gather(proj_weight.astype(jnp.bfloat16), "dp", axis=1, tiled=True),
+        ring_gather(proj_weight.astype(jnp.bfloat16), "dp", 1),
         lax.all_gather(out_weight.astype(jnp.bfloat16), "dp", axis=1, tiled=True),
         lax.all_gather(up_weight.astype(jnp.bfloat16), "dp", axis=1, tiled=True),
         lax.all_gather(down_weight.astype(jnp.bfloat16), "dp", axis=1, tiled=True),

time: 1750 us -> 1770 us (1.011)
  waiting for transfers between devices: 1190 us -> 1120 us
  starting transfers between devices: 0.8 us -> 59.4 us
  local copies, waits for them, and re-layouts: 86.9 us -> 116 us
    all_gather x1 -> x0, waiting for transfers between devices: 72.2 us -> none  [local(): lax.all_gather(proj_weight.astype(jnp.bfloat16), 'dp', axis=1, tiled=True)]
    ppermute x0 -> x15, starting transfers between devices: none -> 58.6 us  [the longest x7 45.6 us: ring_gather(): upper.append(lax.ppermute(upper[-1] if upper else x, axis, back))]
    ppermute x0 -> x15, waiting for transfers between devices: none -> 27.2 us  [the longest x8 20.2 us: ring_gather(): lower.append(lax.ppermute(lower[-1] if lower else x, axis, pairs))]
    all_gather x1, waiting for transfers between devices: 26.5 us -> 0.01 us  [local(): lax.all_gather(out_weight.astype(jnp.bfloat16), 'dp', axis=1, tiled=True)]
  transfers between devices with their start and end apart: 14 -> 28, of which waited for: 13 -> 20; matrix products, arithmetic and copies ran while one was open for 8% -> 9% of each run, Pallas kernels for 0% -> 0%
where the time goes in v1:
time: 1770 us; the launch traced here: 1760 us
  waiting for transfers between devices  1120 us (63%)
  matrix products  237 us (13%)
  other arithmetic  123 us (7%)
  local copies, waits for them, and re-layouts  116 us (7%)
  blocking collectives  81.9 us (5%)
  starting transfers between devices  59.4 us (3%)
  between operations  21 us (1%)
    psum x1, waiting for transfers between devices, local(): lax.psum((big_totals[0], big_totals[1], big_totals[2], big_totals[3]), 'dp')  737 us
    psum x1, waiting for transfers between devices, local(): lax.psum((square_part, weight_square, small_partial), ('dp', 'tensor'))  114 us
    all_gather x1, waiting for transfers between devices, local(): lax.all_gather(up_weight.astype(jnp.bfloat16), 'dp', axis=1, tiled=True)  82.3 us
    all_gather x1, waiting for transfers between devices, local(): lax.all_gather(down_weight.astype(jnp.bfloat16), 'dp', axis=1, tiled=True)  61.7 us
    ppermute x7, starting transfers between devices, ring_gather(): upper.append(lax.ppermute(upper[-1] if upper else x, axis, back))  45.6 us
    psum x1, blocking collectives, local(): lax.psum((square_part, weight_square, small_partial), ('dp', 'tensor'))  42.6 us
    dot_general x2, matrix products, local(): jnp.einsum('td,df->tf', first_low, up_full[layer_at], preferred_element_t...  39.5 us
    psum x1, blocking collectives, local(): update_square = lax.psum(update_square, ('dp', 'tensor'))  39.3 us
  transfers between devices with their start and end apart: 28, of which 20 were waited for; matrix products, arithmetic and copies ran while one was open for 9% of the time, Pallas kernels for 0%

profile of v1, /device:TPU:0, one launch (start us, length us, event | category | flops | bytes accessed | tf_op | source)
XLA Modules:
  0.0 1757.4 jit_solution(4504972746224771627)
XLA Ops:
  11.3 9.4 collective-permute-done
  20.7 5.6 collective-permute-start.8
  26.4 4.7 collective-permute-done.1
  44.7 6.4 collective-permute-start.10
  55.1 7.2 collective-permute-start.11
  66.8 8.9 collective-permute-start.12
  80.5 7.2 collective-permute-start.13
  93.9 6.1 collective-permute-start.14
  138.8 12.9 while.54
  161.9 17.0 all-reduce.13.cloned.1.call-done
  181.9 82.3 %all-gather.6.cloned.1.call-done = bf16[2,768,1536]{2,1,0:T(8,128)(2,1)} async-done(((bf16[2,48,1536]{2,1,0:T(8,128)(2,1)}), bf16[2,768,1536]{2,1,0:T(8,128)(2,1)}) %all-gather.6.cloned.1.call-update) | async-done | bytes 4718608 | tf_op jit(solution)/shard_map/all_gather | solution.py:161
  264.2 20.9 %multiply_convert_fusion.1 = (bf16[1024,1536]{1,0:T(8,128)(2,1)}, f32[1024,1536]{1,0:T(8,128)}, f32[1024,1536]{1,0:T(8,128)}) fusion(f32[1536]{0:T(1024)S(1)} %dynamic-slice_reduce_fusion.5, bf16[2,768,1536]{2,1,0:T(8,128)(2,1)} %all-gather.6.cloned.1.call-done, f32[768]{0:T(1024)S(1)} %copy-done.101, f32[768]{0:T(1024)S(1)} %get-tuple-element.490, ...), kind=kOutput, calls=%fused_computation.156 | convolution fusion | flops 2526806016 | bytes 21257216 | tf_op jit(solution)/shard_map/td,df->tf/dot_general | solution.py:212
  285.1 61.7 %all-gather.8.cloned.1.call-done = bf16[2,768,1536]{2,1,0:T(8,128)(2,1)} async-done(((bf16[2,48,1536]{2,1,0:T(8,128)(2,1)}), bf16[2,768,1536]{2,1,0:T(8,128)(2,1)}) %all-gather.8.cloned.1.call-update) | async-done | bytes 4718608 | tf_op jit(solution)/shard_map/all_gather | solution.py:162
  346.8 6.4 fusion.151
  356.2 16.2 all-reduce.15.cloned.1.call-done
  395.8 14.0 while.55
  415.1 21.7 %all-reduce.17.cloned.1.call-done = bf16[1024,768]{1,0:T(8,128)(2,1)} async-done(((bf16[1024,768]{1,0:T(8,128)(2,1)}), bf16[1024,768]{1,0:T(8,128)(2,1)}) %all-reduce.17.cloned.1.call-update) | async-done | bytes 1572880 | tf_op jit(solution)/shard_map/psum | solution.py:203
  441.2 18.7 %multiply_convert_fusion = (bf16[1024,1536]{1,0:T(8,128)(2,1)S(1)}, f32[1024,1536]{1,0:T(8,128)}, f32[1024,1536]{1,0:T(8,128)}) fusion(f32[1536]{0:T(1024)S(1)} %dynamic-slice_reduce_fusion.4, bf16[2,768,1536]{2,1,0:T(8,128)(2,1)S(1)} %bitcast.453, f32[1024,768]{1,0:T(8,128)S(1)} %get-tuple-element.603, f32[768]{0:T(1024)S(1)} %copy-done.105, ...), kind=kOutput, calls=%fused_computation.143 | convolution fusion | flops 2523660288 | bytes 21258240 | tf_op jit(solution)/shard_map/td,df->tf/dot_general | solution.py:212
  461.7 5.4 fusion.149
  467.2 21.7 %all-reduce.19.cloned.1.call-done = bf16[1024,768]{1,0:T(8,128)(2,1)} async-done(((bf16[1024,768]{1,0:T(8,128)(2,1)}), bf16[1024,768]{1,0:T(8,128)(2,1)}) %all-reduce.19.cloned.1.call-update) | async-done | bytes 1572880 | tf_op jit(solution)/shard_map/psum | solution.py:216
  499.5 9.5 fusion.214
  518.7 8.0 convolution_bitcast_fusion.2
  526.7 9.5 all-reduce.21.cloned.1.call-done
  536.2 4.9 multiply_reduce_fusion.3
  556.2 36.1 %while.56 = (s32[]{:T(128)}, bf16[2,512,6,64]{1,3,2,0:T(8,128)(2,1)}, bf16[2,512,6,64]{1,3,2,0:T(8,128)(2,1)}, f32[2,512,6,64]{1,3,2,0:T(8,128)}, f32[2,6,512,51...) while((s32[]{:T(128)}, ...), condition=%wide.region_27.28_spmd, body=%wide.region_25.27_spmd.sunk | while | flops 1227224064 | bytes 94064864 | solution.py:298
  607.0 5.6 bitcast_convert_fusion.1
  612.7 7.9 convolution_bitcast_fusion
  623.6 4.5 convolution_bitcast_fusion.5
  628.0 6.4 all-reduce.23.cloned.1.call-done
  634.4 5.4 multiply_reduce_fusion.4
  641.8 9.6 fusion.215
  656.9 5.6 convolution_bitcast_fusion.1
  662.6 7.4 pad_maximum_fusion.1
  670.1 4.8 convolution_bitcast_fusion.3
  678.6 4.8 multiply_reduce_fusion.5
  691.4 54.4 %while.57 = (s32[]{:T(128)}, bf16[2,512,6,64]{1,3,2,0:T(8,128)(2,1)}, bf16[2,512,6,64]{1,3,2,0:T(8,128)(2,1)}, f32[2,512,6,64]{1,3,2,0:T(8,128)}, bf16[2,512,6,6...) while((s32[]{:T(128)}, ...), condition=%wide.region_36.37_spmd, body=%wide.region_34.36_spmd.sunk | while | flops 1222512128 | bytes 87736576 | solution.py:298
  691.4 5.2 exponential_select_fusion.3
  696.6 7.6 fusion.317
  704.2 7.8 fusion.318
  718.5 5.2 exponential_select_fusion.3
  723.7 7.6 fusion.317
  731.3 7.8 fusion.318
  755.9 5.0 bitcast_convert_fusion
  761.3 8.5 pad_maximum_fusion
  788.2 736.6 %all-reduce.31.cloned.1.call-done = (f32[2,768,3,384]{3,1,2,0:T(8,128)}, f32[2,768,384]{2,1,0:T(8,128)}, f32[2,768,1536]{2,1,0:T(8,128)}, f32[2,768,1536]{2,1,0:T(8,128)}) async-done(((f32[2,768,3,384]{3,1,2,0:T(8,128)}, f32[2,768,384]{2,1,0:T(8,128)}, f32[2,768,1536]{2,1,0:T(8,128)}, f32[2,768,1536]{2,1,0:T(8,128)}), (f32[2,768,3,384]{3,1,2,0:T(8,128)}, f32[2,768,384]{2,1,0:T(8,128)}, ...) | async-done | bytes 28311568 | tf_op jit(solution)/shard_map/psum | solution.py:345
  1534.4 114.2 %all-reduce.29.cloned.1.call-done = f32[2,8448]{1,0:T(2,128)} async-done(((f32[2,8448]{1,0:T(2,128)}), f32[2,8448]{1,0:T(2,128)}) %all-reduce.29.cloned.1.call-update) | async-done | bytes 67600 | tf_op jit(solution)/shard_map/psum | solution.py:359
  1650.1 42.6 %psum.124 = f32[]{:T(128)} all-reduce(f32[]{:T(128)S(6)} %add.450), channel_id=1, replica_groups=mesh['dp'=16,'tensor'=2] {'dp','tensor'}, use_global_device_ids=true, to_apply=%region_46.47 | all-reduce | flops 1 | bytes 8 | tf_op jit(solution)/shard_map/psum | solution.py:359
  1703.8 39.3 %all-reduce = (f32[4,2]{1,0:T(4,128)S(1)}, f32[4,2]{1,0:T(4,128)S(1)}) all-reduce(f32[4,2]{1,0:T(4,128)S(1)} %pad_maximum_fusion.12, f32[4,2]{1,0:T(4,128)S(1)} %pad_maximum_fusion.11), channel_id=1, replica_groups=mesh['dp'=16,'tensor'=2] {'dp','tensor'}, use_global_device_ids=true, to_apply=%region_74.75 | all-reduce | flops 16 | bytes 128 | tf_op jit(solution)/shard_map/psum | solution.py:375
  (595 shorter events, 326.8 us)
Async XLA Ops:
  7.2 98.5 %copy-start.28 = (f32[2,48,3,384]{3,1,2,0:T(8,128)S(1)}, f32[2,48,3,384]{3,1,2,0:T(8,128)}, u32[]{:S(2)}) copy-start(f32[2,48,3,384]{3,1,2,0:T(8,128)} %param.29) | copy-start | bytes 1327108
  7.2 147.5 %all-gather.4.cloned.1.call-start = ((), (), s32[]{:S(2)}) async-start(), calls=%async_computation | async-start | bytes 1253376 | tf_op jit(solution)/shard_map/all_gather | solution.py:160
  8.3 12.4 collective-permute-start
  20.7 10.3 collective-permute-start.1
  20.7 14.1 collective-permute-start.8
  31.1 11.1 collective-permute-start.2
  34.8 9.9 collective-permute-start.9
  42.2 9.6 collective-permute-start.3
  44.7 10.4 collective-permute-start.10
  51.8 10.5 collective-permute-start.4
  54.6 124.3 %all-reduce.13.cloned.1.call-start = ((), (), s32[]{:S(2)}) async-start(), calls=%async_computation.1 | async-start | bytes 3145728 | tf_op jit(solution)/shard_map/psum | solution.py:203
  55.1 11.6 collective-permute-start.11
  62.3 13.4 collective-permute-start.5
  64.1 308.4 %copy-start.74 = (f32[768]{0:T(1024)}, f32[768]{0:T(1024)S(1)}, u32[]{:S(2)}) copy-start(f32[768]{0:T(1024)S(1)} %get-tuple-element.491) | copy-start | bytes 9220
  64.1 308.4 %copy-start.83 = (f32[768]{0:T(1024)}, f32[768]{0:T(1024)S(1)}, u32[]{:S(2)}) copy-start(f32[768]{0:T(1024)S(1)} %get-tuple-element.490) | copy-start | bytes 9220
  64.1 372.7 %copy-start.87 = (f32[768]{0:T(1024)}, f32[768]{0:T(1024)S(1)}, u32[]{:S(2)}) copy-start(f32[768]{0:T(1024)S(1)} %get-tuple-element.487) | copy-start | bytes 9220
  66.8 13.7 collective-permute-start.12
  75.7 14.0 collective-permute-start.6
  80.5 13.4 collective-permute-start.13
  89.7 10.3 collective-permute-start.7
  93.9 16.8 collective-permute-start.14
  158.2 106.0 %all-gather.6.cloned.1.call-start = ((), (), s32[]{:S(2)}) async-start(), calls=%async_computation.2 | async-start | bytes 5013504 | tf_op jit(solution)/shard_map/all_gather | solution.py:161
  160.1 186.7 %all-gather.8.cloned.1.call-start = ((), (), s32[]{:S(2)}) async-start(), calls=%async_computation.3 | async-start | bytes 5013504 | tf_op jit(solution)/shard_map/all_gather | solution.py:162
  160.9 211.5 %all-reduce.15.cloned.1.call-start = ((), (), s32[]{:S(2)}) async-start(), calls=%async_computation.4 | async-start | bytes 3145728 | tf_op jit(solution)/shard_map/psum | solution.py:216
  161.9 102.3 %copy-start.119 = (f32[1536]{0:T(1024)}, f32[1536]{0:T(1024)S(1)}, u32[]{:S(2)}) copy-start(f32[1536]{0:T(1024)S(1)} %dynamic-slice_reduce_fusion.5) | copy-start | bytes 18436
  178.9 85.3 %copy-start.101 = (f32[768]{0:T(1024)S(1)}, f32[768]{0:T(1024)}, u32[]{:S(2)}) copy-start(f32[768]{0:T(1024)} %get-tuple-element.489) | copy-start | bytes 9220
  181.0 191.4 %copy-start.77 = (f32[1024]{0:T(1024)}, f32[1024]{0:T(1024)S(1)}, u32[]{:S(2)}) copy-start(f32[1024]{0:T(1024)S(1)} %broadcast_multiply_fusion.3) | copy-start | bytes 12292
  181.9 103.2 %copy-start.93 = (f32[1024]{0:T(1024)}, f32[1024]{0:T(1024)S(1)}, u32[]{:S(2)}) copy-start(f32[1024]{0:T(1024)S(1)} %multiply_reduce_fusion.13) | copy-start | bytes 12292
  181.9 190.5 %copy-start.85 = (f32[1024]{0:T(1024)}, f32[1024]{0:T(1024)S(1)}, u32[]{:S(2)}) copy-start(f32[1024]{0:T(1024)S(1)} %fusion.166) | copy-start | bytes 12292
  353.2 83.6 %all-reduce.17.cloned.1.call-start = ((), (), s32[]{:S(2)}) async-start(), calls=%async_computation.5 | async-start | bytes 3145728 | tf_op jit(solution)/shard_map/psum | solution.py:203
  376.1 60.7 %copy-start.79 = (f32[1024]{0:T(1024)}, f32[1024]{0:T(1024)S(1)}, u32[]{:S(2)}) copy-start(f32[1024]{0:T(1024)S(1)} %broadcast_multiply_fusion.2) | copy-start | bytes 12292
  376.7 60.1 %copy-start.90 = (f32[1024]{0:T(1024)}, f32[1024]{0:T(1024)S(1)}, u32[]{:S(2)}) copy-start(f32[1024]{0:T(1024)S(1)} %fusion.167) | copy-start | bytes 12292
  411.8 25.0 %copy-start.107 = (f32[768]{0:T(1024)S(1)}, f32[768]{0:T(1024)}, u32[]{:S(2)}) copy-start(f32[768]{0:T(1024)} %get-tuple-element.485) | copy-start | bytes 9220
  415.1 73.8 %all-reduce.19.cloned.1.call-start = ((), (), s32[]{:S(2)}) async-start(), calls=%async_computation.6 | async-start | bytes 3145728 | tf_op jit(solution)/shard_map/psum | solution.py:216
  461.7 27.2 %copy-start.106 = (f32[768]{0:T(1024)S(1)}, f32[768]{0:T(1024)}, u32[]{:S(2)}) copy-start(f32[768]{0:T(1024)} %get-tuple-element.482) | copy-start | bytes 9220
  467.1 69.1 %all-reduce.21.cloned.1.call-start = ((), (), s32[]{:S(2)}) async-start(), calls=%async_computation.7 | async-start | bytes 3145728 | tf_op jit(solution)/shard_map/psum | solution.py:268
  514.5 119.9 %all-reduce.23.cloned.1.call-start = ((), (), s32[]{:S(2)}) async-start(), calls=%async_computation.8 | async-start | bytes 3145728 | tf_op jit(solution)/shard_map/psum | solution.py:315
  612.7 65.9 %all-reduce.25.cloned.1.call-start = ((), (), s32[]{:S(2)}) async-start(), calls=%async_computation.9 | async-start | bytes 3145728 | tf_op jit(solution)/shard_map/psum | solution.py:268
  656.8 126.8 %all-reduce.27.cloned.1.call-start = ((), (), s32[]{:S(2)}) async-start(), calls=%async_computation.10 | async-start | bytes 3145728 | tf_op jit(solution)/shard_map/psum | solution.py:315
  761.0 763.8 %all-reduce.31.cloned.1.call-start = ((), (), s32[]{:S(2)}) async-start(), calls=%async_computation.12 | async-start | bytes 56623104 | tf_op jit(solution)/shard_map/psum | solution.py:345
  780.0 868.6 %all-reduce.29.cloned.1.call-start = ((), (), s32[]{:S(2)}) async-start(), calls=%async_computation.11 | async-start | bytes 135168 | tf_op jit(solution)/shard_map/psum | solution.py:359
  783.6 910.5 %copy-start.51 = (f32[2,48,384]{2,1,0:T(8,128)S(1)}, f32[2,48,384]{2,1,0:T(8,128)}, u32[]{:S(2)}) copy-start(f32[2,48,384]{2,1,0:T(8,128)} %param.30) | copy-start | bytes 442372
  787.3 908.7 %copy-start.36 = (f32[2,48,1536]{2,1,0:T(8,128)S(1)}, f32[2,48,1536]{2,1,0:T(8,128)}, u32[]{:S(2)}) copy-start(f32[2,48,1536]{2,1,0:T(8,128)} %param.31) | copy-start | bytes 1769476
  787.3 908.7 %copy-start.67 = (f32[2,48,1536]{2,1,0:T(8,128)S(1)}, f32[2,48,1536]{2,1,0:T(8,128)}, u32[]{:S(2)}) copy-start(f32[2,48,1536]{2,1,0:T(8,128)} %param.38) | copy-start | bytes 1769476
  1524.8 173.3 %copy-start.35 = (f32[2,48,1536]{2,1,0:T(8,128)S(1)}, f32[2,48,1536]{2,1,0:T(8,128)}, u32[]{:S(2)}) copy-start(f32[2,48,1536]{2,1,0:T(8,128)} %param.32) | copy-start | bytes 1769476
  1698.0 47.4 %copy-start.43 = (f32[2,48,1536]{2,1,0:T(8,128)}, f32[2,48,1536]{2,1,0:T(8,128)S(1)}, u32[]{:S(2)}) copy-start(f32[2,48,1536]{2,1,0:T(8,128)S(1)} %get-tuple-element.586) | copy-start | bytes 1769476
  1698.0 47.4 %copy-start.44 = (f32[2,48,1536]{2,1,0:T(8,128)}, f32[2,48,1536]{2,1,0:T(8,128)S(1)}, u32[]{:S(2)}) copy-start(f32[2,48,1536]{2,1,0:T(8,128)S(1)} %get-tuple-element.587) | copy-start | bytes 1769476
  1701.2 45.4 %copy-start.45 = (f32[2,48,1536]{2,1,0:T(8,128)}, f32[2,48,1536]{2,1,0:T(8,128)S(1)}, u32[]{:S(2)}) copy-start(f32[2,48,1536]{2,1,0:T(8,128)S(1)} %get-tuple-element.588) | copy-start | bytes 1769476
  (129 other events, 632.0 us)
Sparse Core Ops, SparseCore 0:
  54.8 59.7 all-gather.3
  158.3 20.5 all-reduce.12
  182.5 81.6 all-gather.5
  267.7 79.0 all-gather.7
  353.4 19.0 all-reduce.14
  415.2 21.5 all-reduce.16
  467.2 21.5 all-reduce.18
  514.6 21.5 all-reduce.20
  612.8 21.5 all-reduce.22
  657.0 21.5 all-reduce.24
  761.1 21.5 all-reduce.26
  789.0 735.7 all-reduce.30
  1531.8 116.6 all-reduce.28
